TPU v7x, 32 devices: a whole 2x2x4 slice. The times are simulated.
32 devices in a mesh: fsdp: 8 (over z, y), rep: 4 (over x, core).
Axes of the slice: x: 2, y: 2, z: 4, core: 2. Of those that a mesh axis runs over, the one named last changes fastest.
Arguments:
- layer_input: bfloat16 [64, 512, 768], P(('fsdp', 'rep')), may hold values from -6 to 6
- segment_ids: int32 [64, 512], P(('fsdp', 'rep')), may hold values from 0 to 511, as said below
- joint_weight: bfloat16 [768, 2304], P('fsdp'), may hold values from -0.21875 to 0.21875
- query_bias: bfloat16 [768], replicated, may hold values from -3 to 3
- value_bias: bfloat16 [768], replicated, may hold values from -3 to 3
- close_weight: bfloat16 [768, 768], P('fsdp'), may hold values from -0.875 to 0.875
- close_bias: bfloat16 [768], replicated, may hold values from -3 to 3
- first_gain: bfloat16 [768], replicated, may hold values from 0.099609375 to 1.8984375
- first_shift: bfloat16 [768], replicated, may hold values from -3 to 3
- expand_weight: bfloat16 [768, 3072], P('fsdp'), may hold values from -0.21875 to 0.21875
- expand_bias: bfloat16 [3072], replicated, may hold values from -3 to 3
- shrink_weight: bfloat16 [3072, 768], P('fsdp'), may hold values from -0.109375 to 0.109375
- shrink_bias: bfloat16 [768], replicated, may hold values from -3 to 3
- second_gain: bfloat16 [768], replicated, may hold values from 0.099609375 to 1.8984375
- second_shift: bfloat16 [768], replicated, may hold values from -3 to 3
- cotangent: bfloat16 [64, 512, 768], P(('fsdp', 'rep')), may hold values from -6 to 6
Outputs:
- layer_output: bfloat16 [64, 512, 768], P(('fsdp', 'rep'))
- input_grad: float32 [64, 512, 768], P(('fsdp', 'rep'))
- joint_grad: float32 [768, 2304], P('fsdp')
- query_bias_grad: float32 [768], replicated
- value_bias_grad: float32 [768], replicated
- close_grad: float32 [768, 768], P('fsdp')
- close_bias_grad: float32 [768], replicated
- first_gain_grad: float32 [768], replicated
- first_shift_grad: float32 [768], replicated
- expand_grad: float32 [768, 3072], P('fsdp')
- expand_bias_grad: float32 [3072], replicated
- shrink_grad: float32 [3072, 768], P('fsdp')
- shrink_bias_grad: float32 [768], replicated
- second_gain_grad: float32 [768], replicated
- second_shift_grad: float32 [768], replicated
Inputs may be any that keep to these rules, and one draw needn't show every extreme that they name: `segment_ids`: along each packed row of 512 positions the document numbers start at 0, never fall and rise by at most one from a position to the next; every position belongs to a document. Some row holds 512 documents of one position.
All inputs are finite; a program needn't handle non-finite values.
Results may differ from a plain program's by a relative error of at most 0.015.
Values may be sent and summed in bfloat16 or wider, within the bound.
No kernel may reach another device: no remote copies, remote signals or barrier semaphores. Data moves between devices by JAX's collectives and lax.ppermute only.
A program may use at most 192 MiB of HBM per device.

v0:
```python
import math
import jax
import jax.numpy as jnp
from jax import lax
from jax.sharding import PartitionSpec as P

HEADS = 12
EPS = 1e-12


def layer_norm(values, gain, shift):
    average = jnp.mean(values, axis=-1, keepdims=True)
    centred = values - average
    variance = jnp.mean(centred * centred, axis=-1, keepdims=True)
    return centred * lax.rsqrt(variance + EPS) * gain + shift


def gelu_exact(values):
    return jax.nn.gelu(values, approximate=False)


def split_heads(packed):
    pos_count = packed.shape[0]
    model_width = packed.shape[1] // 3
    head_size = model_width // HEADS
    queries = packed[:, :model_width].reshape(pos_count, HEADS, head_size)
    keys_part = packed[:, model_width : 2 * model_width].reshape(pos_count, HEADS, head_size)
    values_part = packed[:, 2 * model_width :].reshape(pos_count, HEADS, head_size)
    return (queries, keys_part, values_part, 1.0 / math.sqrt(head_size))


def masked_scores(queries, keys_part, segments, score_scale):
    scores = (
        jnp.einsum("qhd,khd->hqk", queries, keys_part, preferred_element_type=jnp.float32)
        * score_scale
    )
    same_doc = segments[:, None] == segments[None, :]
    return jnp.where(same_doc[None], scores, -jnp.inf)


def attend_row(packed, segments):
    queries, keys_part, values_part, score_scale = split_heads(packed)
    scores = masked_scores(queries, keys_part, segments, score_scale)
    top_score = jnp.max(scores, axis=-1, keepdims=True)
    raised = jnp.exp(scores - top_score)
    denominator = jnp.sum(raised, axis=-1, keepdims=True)
    attn_low = (raised / denominator).astype(jnp.bfloat16)
    context = jnp.einsum("hqk,khd->qhd", attn_low, values_part, preferred_element_type=jnp.float32)
    return (
        context.reshape(packed.shape[0], packed.shape[1] // 3),
        top_score + jnp.log(denominator),
    )


def attend_back(packed, segments, log_total, grad_context):
    pos_count = packed.shape[0]
    model_width = packed.shape[1] // 3
    queries, keys_part, values_part, score_scale = split_heads(packed)
    scores = masked_scores(queries, keys_part, segments, score_scale)
    attn_weights = jnp.exp(scores - log_total)
    grad_heads = grad_context.reshape(pos_count, HEADS, model_width // HEADS)
    grad_attn = jnp.einsum(
        "qhd,khd->hqk", grad_heads, values_part, preferred_element_type=jnp.float32
    )
    inner_sum = jnp.sum(grad_attn * attn_weights, axis=-1, keepdims=True)
    grad_scores = (attn_weights * (grad_attn - inner_sum)).astype(jnp.bfloat16)
    grad_queries = (
        jnp.einsum("hqk,khd->qhd", grad_scores, keys_part, preferred_element_type=jnp.float32)
        * score_scale
    )
    grad_keys = (
        jnp.einsum("hqk,qhd->khd", grad_scores, queries, preferred_element_type=jnp.float32)
        * score_scale
    )
    grad_values = jnp.einsum(
        "hqk,qhd->khd",
        attn_weights.astype(jnp.bfloat16),
        grad_heads,
        preferred_element_type=jnp.float32,
    )
    return jnp.concatenate(
        [
            grad_queries.reshape(pos_count, model_width),
            grad_keys.reshape(pos_count, model_width),
            grad_values.reshape(pos_count, model_width),
        ],
        axis=1,
    )


def body(
    layer_input,
    segment_ids,
    joint_weight,
    query_bias,
    value_bias,
    close_weight,
    close_bias,
    first_gain,
    first_shift,
    expand_weight,
    expand_bias,
    shrink_weight,
    shrink_bias,
    second_gain,
    second_shift,
    cotangent,
):
    row_count, pos_count, model_width = layer_input.shape
    tok_count = row_count * pos_count
    flat_input = layer_input.reshape(tok_count, model_width)
    joint_full, close_full = (
        lax.all_gather(joint_weight, "fsdp", axis=0, tiled=True),
        lax.all_gather(close_weight, "fsdp", axis=0, tiled=True),
    )
    joint_bias = jnp.concatenate([query_bias, jnp.zeros_like(query_bias), value_bias]).astype(
        jnp.float32
    )
    mixed = jnp.dot(flat_input, joint_full, preferred_element_type=jnp.float32) + joint_bias
    joint_low = mixed.astype(jnp.bfloat16).reshape(row_count, pos_count, 3 * model_width)
    context, log_total = lax.map(
        lambda packet: attend_row(packet[0], packet[1]), (joint_low, segment_ids)
    )
    context_low = context.reshape(tok_count, model_width).astype(jnp.bfloat16)
    expand_full, shrink_full = (
        lax.all_gather(expand_weight, "fsdp", axis=0, tiled=True),
        lax.all_gather(shrink_weight, "fsdp", axis=0, tiled=True),
    )
    branch = jnp.dot(
        context_low, close_full, preferred_element_type=jnp.float32
    ) + close_bias.astype(jnp.float32)
    first_sum = flat_input.astype(jnp.float32) + branch
    hidden, first_pull = jax.vjp(
        layer_norm, first_sum, first_gain.astype(jnp.float32), first_shift.astype(jnp.float32)
    )
    hidden_low = hidden.astype(jnp.bfloat16)
    inner = jnp.dot(
        hidden_low, expand_full, preferred_element_type=jnp.float32
    ) + expand_bias.astype(jnp.float32)
    active, gelu_pull = jax.vjp(gelu_exact, inner)
    active_low = active.astype(jnp.bfloat16)
    ffn_out = jnp.dot(
        active_low, shrink_full, preferred_element_type=jnp.float32
    ) + shrink_bias.astype(jnp.float32)
    output, second_pull = jax.vjp(
        layer_norm,
        hidden + ffn_out,
        second_gain.astype(jnp.float32),
        second_shift.astype(jnp.float32),
    )
    layer_output = output.astype(jnp.bfloat16).reshape(row_count, pos_count, model_width)
    expand_back, shrink_back = (
        lax.all_gather(expand_weight, "fsdp", axis=0, tiled=True),
        lax.all_gather(shrink_weight, "fsdp", axis=0, tiled=True),
    )
    grad_second, second_gain_part, second_shift_part = second_pull(
        cotangent.reshape(tok_count, model_width).astype(jnp.float32)
    )
    grad_ffn = grad_second.astype(jnp.bfloat16)
    shrink_term = jnp.einsum("tf,td->fd", active_low, grad_ffn, preferred_element_type=jnp.float32)
    grad_active = jnp.einsum("td,fd->tf", grad_ffn, shrink_back, preferred_element_type=jnp.float32)
    grad_inner = gelu_pull(grad_active)[0].astype(jnp.bfloat16)
    expand_term = jnp.einsum(
        "td,tf->df", hidden_low, grad_inner, preferred_element_type=jnp.float32
    )
    grad_hidden = grad_second + jnp.einsum(
        "tf,df->td", grad_inner, expand_back, preferred_element_type=jnp.float32
    )
    expand_part, shrink_part = (
        lax.psum_scatter(expand_term, "fsdp", scatter_dimension=0, tiled=True),
        lax.psum_scatter(shrink_term, "fsdp", scatter_dimension=0, tiled=True),
    )
    grad_first, first_gain_part, first_shift_part = first_pull(grad_hidden)
    grad_branch = grad_first.astype(jnp.bfloat16)
    joint_back, close_back = (
        lax.all_gather(joint_weight, "fsdp", axis=0, tiled=True),
        lax.all_gather(close_weight, "fsdp", axis=0, tiled=True),
    )
    close_term = jnp.einsum(
        "td,te->de", context_low, grad_branch, preferred_element_type=jnp.float32
    )
    grad_context = jnp.einsum(
        "te,de->td", grad_branch, close_back, preferred_element_type=jnp.float32
    ).astype(jnp.bfloat16)
    grad_mixed = lax.map(
        lambda packet: attend_back(packet[0], packet[1], packet[2], packet[3]),
        (
            joint_low,
            segment_ids,
            log_total,
            grad_context.reshape(row_count, pos_count, model_width),
        ),
    )
    grad_mixed_low = grad_mixed.reshape(tok_count, 3 * model_width).astype(jnp.bfloat16)
    joint_term = jnp.einsum(
        "td,te->de", flat_input, grad_mixed_low, preferred_element_type=jnp.float32
    )
    input_grad = grad_first + jnp.einsum(
        "te,de->td", grad_mixed_low, joint_back, preferred_element_type=jnp.float32
    )
    joint_part, close_part = (
        lax.psum_scatter(joint_term, "fsdp", scatter_dimension=0, tiled=True),
        lax.psum_scatter(close_term, "fsdp", scatter_dimension=0, tiled=True),
    )
    joint_grad, close_grad, expand_grad, shrink_grad = (
        lax.psum(joint_part.astype(jnp.bfloat16), "rep").astype(jnp.float32),
        lax.psum(close_part.astype(jnp.bfloat16), "rep").astype(jnp.float32),
        lax.psum(expand_part.astype(jnp.bfloat16), "rep").astype(jnp.float32),
        lax.psum(shrink_part.astype(jnp.bfloat16), "rep").astype(jnp.float32),
    )
    grad_mixed_wide = grad_mixed_low.astype(jnp.float32)
    vector_terms = (
        jnp.sum(grad_mixed_wide[:, :model_width], axis=0),
        jnp.sum(grad_mixed_wide[:, 2 * model_width :], axis=0),
        jnp.sum(grad_branch.astype(jnp.float32), axis=0),
        first_gain_part,
        first_shift_part,
        jnp.sum(grad_inner.astype(jnp.float32), axis=0),
        jnp.sum(grad_ffn.astype(jnp.float32), axis=0),
        second_gain_part,
        second_shift_part,
    )
    (
        query_bias_grad,
        value_bias_grad,
        close_bias_grad,
        first_gain_grad,
        first_shift_grad,
        expand_bias_grad,
        shrink_bias_grad,
        second_gain_grad,
        second_shift_grad,
    ) = lax.psum(
        (
            vector_terms[0],
            vector_terms[1],
            vector_terms[2],
            vector_terms[3],
            vector_terms[4],
            vector_terms[5],
            vector_terms[6],
            vector_terms[7],
            vector_terms[8],
        ),
        ("fsdp", "rep"),
    )
    return (
        layer_output,
        input_grad.reshape(row_count, pos_count, model_width),
        joint_grad,
        query_bias_grad,
        value_bias_grad,
        close_grad,
        close_bias_grad,
        first_gain_grad,
        first_shift_grad,
        expand_grad,
        expand_bias_grad,
        shrink_grad,
        shrink_bias_grad,
        second_gain_grad,
        second_shift_grad,
    )


def solution(mesh):
    placed = (
        P(("fsdp", "rep"), None, None),
        P(("fsdp", "rep"), None),
        P("fsdp", None),
        P(),
        P(),
        P("fsdp", None),
        P(),
        P(),
        P(),
        P("fsdp", None),
        P(),
        P("fsdp", None),
        P(),
        P(),
        P(),
        P(("fsdp", "rep"), None, None),
    )
    return jax.shard_map(
        body,
        mesh=mesh,
        in_specs=placed,
        out_specs=(
            P(("fsdp", "rep"), None, None),
            P(("fsdp", "rep"), None, None),
            P("fsdp", None),
            P(),
            P(),
            P("fsdp", None),
            P(),
            P(),
            P(),
            P("fsdp", None),
            P(),
            P("fsdp", None),
            P(),
            P(),
            P(),
        ),
        check_vma=False,
    )
```

profile of v0, /device:TPU:0, one launch (start us, length us, event | category | flops | bytes accessed | tf_op | source)
XLA Modules:
  0.0 939.9 jit_solution(8562727655183991149)
XLA Ops:
  19.7 57.8 %all-gather.5.cloned.1.call-done = bf16[768,2304]{1,0:T(8,128)(2,1)} async-done(((bf16[96,2304]{1,0:T(8,128)(2,1)}), bf16[768,2304]{1,0:T(8,128)(2,1)}) %all-gather.5.cloned.1.call-update) | async-done | bytes 3538960 | tf_op jit(solution)/shard_map/all_gather | solution.py:113
  77.5 8.4 add_convert_fusion.1
  86.0 6.8 copy.54
  92.8 23.4 %while.22 = (s32[]{:T(128)}, bf16[2,512,768]{2,1,0:T(8,128)(2,1)}, f32[2,12,512,1]{2,1,3,0:T(8,128)S(1)}, bf16[2,512,2304]{1,2,0:T(8,128)(2,1)}, s32[2,512]{1,0:T(2,128)S(1)}, /*index=5*/s32[]{:T(128)}) while((s32[]{:T(128)}, bf16[2,512,768]{2,1,0:T(8,128)(2,1)}, f32[2,12,512,1]{2,1,3,0:T(8,128)S(1)}, bf16[2,512,2304]{1,2,0:T(8,128)(2,1)}, ...), condition=%wide.region_3.4_spmd, body=%wide.region_0.3_spmd.sunk | while | flops 843311104 | bytes 54753372 | solution.py:121
  99.6 3.6 fusion.98
  111.3 3.6 fusion.98
  116.2 3.4 all-gather.7.cloned.1.call-done
  119.6 3.8 fusion.33
  124.0 75.9 %all-gather.9.cloned.1.call-done = bf16[768,3072]{1,0:T(8,128)(2,1)} async-done(((bf16[96,3072]{1,0:T(8,128)(2,1)}), bf16[768,3072]{1,0:T(8,128)(2,1)}) %all-gather.9.cloned.1.call-update) | async-done | bytes 4718608 | tf_op jit(solution)/shard_map/all_gather | solution.py:126
  199.8 36.0 %multiply_convert_fusion.1 = (bf16[1024,3072]{1,0:T(8,128)(2,1)}, f32[1024,3072]{1,0:T(8,128)}, f32[1024,3072]{1,0:T(8,128)}) fusion(f32[3072]{0:T(1024)S(1)} %copy-done.28, bf16[768,3072]{1,0:T(8,128)(2,1)} %all-gather.9.cloned.1.call-done, f32[1024,768]{1,0:T(8,128)S(1)} %get-tuple-element.220, f32[768]{0:T(1024)S(1)} %copy-done.19, ...), kind=kOutput, calls=%fused_computation.34 | convolution fusion | flops 5043388416 | bytes 39348224 | tf_op jit(solution)/shard_map/dot_general | solution.py:137
  235.8 43.8 %all-gather.11.cloned.1.call-done = bf16[3072,768]{1,0:T(8,128)(2,1)} async-done(((bf16[384,768]{1,0:T(8,128)(2,1)}), bf16[3072,768]{1,0:T(8,128)(2,1)}) %all-gather.11.cloned.1.call-update) | async-done | bytes 4718608 | tf_op jit(solution)/shard_map/all_gather | solution.py:127
  279.6 8.9 fusion.34
  295.5 19.4 %convert_reduce_fusion = (f32[3072]{0:T(1024)}, bf16[1024,3072]{1,0:T(8,128)(2,1)}) fusion(f32[1024,3072]{1,0:T(8,128)} %get-tuple-element.207, bf16[1024,768]{1,0:T(8,128)(2,1)} %get-tuple-element.199, bf16[3072,768]{1,0:T(8,128)(2,1)} %all-gather.11.cloned.1.call-done, f32[1024,3072]{1,0:T(8,128)} %get-tuple-element.221, f32[3072]{0:T(1024)S(1)} %copy-done.28), kind=kOutput, calls=%fused_computation.32 | convolution fusion | flops 4885312512 | bytes 37773312 | tf_op jit(solution)/shard_map/td,fd->tf/dot_general | solution.py:161
  315.0 10.1 %multiply_reduce_fusion.1 = (f32[768]{0:T(1024)}, f32[1024]{0:T(1024)S(1)}, f32[768]{0:T(1024)}, f32[1024,768]{1,0:T(8,128)S(1)}) fusion(f32[1024,768]{1,0:T(8,128)S(1)} %get-tuple-element.220, f32[1024]{0:T(1024)S(1)} %fusion.22, f32[1024]{0:T(1024)S(1)} %broadcast_multiply_fusion.1, f32[768]{0:T(1024)S(1)} %copy-done.15, ...), kind=kOutput, calls=%fused_computation.62 | convolution fusion | flops 4839699456 | bytes 20472832 | tf_op jit(solution)/shard_map/tf,df->td/dot_general | solution.py:166
  334.9 62.1 %while.23 = (s32[]{:T(128)}, bf16[2,512,2304]{2,1,0:T(8,128)(2,1)}, bf16[2,512,2304]{1,2,0:T(8,128)(2,1)}, s32[2,512]{1,0:T(2,128)S(1)}, f32[2,12,512,1]{2,1,3,0...) while((s32[]{:T(128)}, bf16[2,512,2304]{2,1,0:T(8,128)(2,1)}, ...), condition=%wide.region_14.15_spmd, body=%wide.region_12.14_spmd.sunk | while | flops 2069358592 | bytes 142784688 | solution.py:185
  339.5 3.2 fusion.111
  342.7 6.9 multiply_reduce_fusion.6
  349.5 7.1 multiply_convert_fusion.3
  362.5 3.3 constant_dynamic-update-slice_fusion.5
  373.4 6.9 multiply_reduce_fusion.6
  380.3 7.2 multiply_convert_fusion.3
  393.4 3.4 constant_dynamic-update-slice_fusion.5
  397.0 9.7 %convolution_bitcast_fusion = f32[768,2304]{0,1:T(8,128)} fusion(bf16[2,512,2304]{2,1,0:T(8,128)(2,1)} %get-tuple-element.77, bf16[2,512,768]{2,1,0:T(8,128)(2,1)} %param.20), kind=kOutput, calls=%fused_computation.49 | convolution fusion | flops 3623878656 | bytes 13369344 | tf_op jit(solution)/shard_map/td,te->de/dot_general | solution.py:195
  406.7 8.1 copy.66
  416.6 10.7 %fusion.24 = f32[768,3072]{1,0:T(8,128)} fusion(bf16[1024,3072]{1,0:T(8,128)(2,1)} %get-tuple-element.226, f32[1024,768]{1,0:T(8,128)S(1)} %copy-done.1, f32[768]{0:T(1024)S(1)} %copy-done.20, f32[768]{0:T(1024)S(1)} %copy-done.16, f32[1024]{0:T(1024)S(1)} %copy-done.14, f32[1024]{0:T(1024)S(1)} %copy-done.12), kind=kOutput, calls=%fused_computation.89 | convolution fusion | flops 4835770368 | bytes 18888704 | tf_op jit(solution)/shard_map/td,tf->df/dot_general | solution.py:163
  428.7 10.2 %fusion.37 = f32[3072,768]{1,0:T(8,128)} fusion(bf16[1024,3072]{1,0:T(8,128)(2,1)} %get-tuple-element.206, bf16[1024,768]{1,0:T(8,128)(2,1)S(1)} %copy-done.8), kind=kOutput, calls=%fused_computation.99 | convolution fusion | flops 4831838208 | bytes 17301504 | tf_op jit(solution)/shard_map/tf,td->fd/dot_general | solution.py:160
  444.5 43.5 %all-reduce = (f32[768]{0:T(1024)}, f32[768]{0:T(1024)}, f32[768]{0:T(1024)}, f32[768]{0:T(1024)}, f32[768]{0:T(1024)}, /*index=5*/f32[3072]{0:T(1024)}, f32[768]{0:T(1024)}, f32[768]{0:T(1024)}, f32[768]{0:T(1024)}) all-reduce(f32[768]{0:T(1024)S(1)} %get-tuple-element.157, ...), channel_id=1, replica_groups=mesh['fsdp'=8,'rep'=4] {'fsdp','rep'}, use_global_device_ids=true, to_apply=%region_18.19 | all-reduce | flops 9216 | bytes 73728 | tf_op jit(solution)/shard_map/psum | solution.py:233
  489.6 54.0 %reduce-scatter.13.cloned.1.call-done = f32[96,2304]{1,0:T(8,128)} async-done(((f32[768,2304]{1,0:T(8,128)}), f32[96,2304]{1,0:T(8,128)}) %reduce-scatter.13.cloned.1.call-update) | async-done | bytes 884752
  545.9 162.6 %reduce-scatter.9.cloned.1.call-done = f32[96,3072]{1,0:T(8,128)} async-done(((f32[768,3072]{1,0:T(8,128)}), f32[96,3072]{1,0:T(8,128)}) %reduce-scatter.9.cloned.1.call-update) | async-done | bytes 1179664 | tf_op jit(solution)/shard_map/reduce_scatter | solution.py:170
  710.6 162.7 %reduce-scatter.11.cloned.1.call-done = f32[384,768]{1,0:T(8,128)} async-done(((f32[3072,768]{1,0:T(8,128)}), f32[384,768]{1,0:T(8,128)}) %reduce-scatter.11.cloned.1.call-update) | async-done | bytes 1179664 | tf_op jit(solution)/shard_map/reduce_scatter | solution.py:171
  875.5 8.9 add_add_fusion.4
  884.5 40.4 %all-reduce.4.cloned.1.call-done = (bf16[96,2304]{0,1:T(8,128)(2,1)}, bf16[96,768]{1,0:T(8,128)(2,1)}, bf16[96,3072]{1,0:T(8,128)(2,1)}, bf16[384,768]{1,0:T(8,128)(2,1)}) async-done(((bf16[96,2304]{0,1:T(8,128)(2,1)}, bf16[96,768]{1,0:T(8,128)(2,1)}, bf16[96,3072]{1,0:T(8,128)(2,1)}, bf16[384,768]{1,0:T(8,128)(2,1)}), (bf16[96,2304]{0,1:T(8,128)(2,1)}, bf16[96,768]{1,0:T(8,128)(2,1)}, ...) | async-done | bytes 1769488 | tf_op jit(solution)/shard_map/psum | solution.py:206
  (176 shorter events, 94.5 us)
Async XLA Ops:
  7.2 70.3 %all-gather.5.cloned.1.call-start = ((), (), s32[]{:S(2)}) async-start(), calls=%async_computation.4 | async-start | bytes 3981312 | tf_op jit(solution)/shard_map/all_gather | solution.py:113
  7.9 111.7 %all-gather.7.cloned.1.call-start = ((), (), s32[]{:S(2)}) async-start(), calls=%async_computation.5 | async-start | bytes 1327104 | tf_op jit(solution)/shard_map/all_gather | solution.py:114
  8.7 191.2 %all-gather.9.cloned.1.call-start = ((), (), s32[]{:S(2)}) async-start(), calls=%async_computation.6 | async-start | bytes 5308416 | tf_op jit(solution)/shard_map/all_gather | solution.py:126
  9.4 270.2 %all-gather.11.cloned.1.call-start = ((), (), s32[]{:S(2)}) async-start(), calls=%async_computation.7 | async-start | bytes 5308416 | tf_op jit(solution)/shard_map/all_gather | solution.py:127
  10.0 478.0 %reduce-scatter.7.cloned.1.call-start = ((), (), s32[]{:S(2)}) async-start(), calls=%async_computation.8 | async-start | bytes 2654208 | tf_op jit(solution)/shard_map/reduce_scatter | solution.py:203
  86.0 6.8 copy-start.17
  92.8 26.8 %copy-start.31 = (f32[768]{0:T(1024)S(1)}, f32[768]{0:T(1024)}, u32[]{:S(2)}) copy-start(f32[768]{0:T(1024)} %convert_element_type.127) | copy-start | bytes 9220
  116.2 3.4 copy-start.9
  119.6 80.2 %copy-start.15 = (f32[768]{0:T(1024)S(1)}, f32[768]{0:T(1024)}, u32[]{:S(2)}) copy-start(f32[768]{0:T(1024)} %convert_element_type.128) | copy-start | bytes 9220
  119.6 80.2 %copy-start.19 = (f32[768]{0:T(1024)S(1)}, f32[768]{0:T(1024)}, u32[]{:S(2)}) copy-start(f32[768]{0:T(1024)} %convert_element_type.129) | copy-start | bytes 9220
  119.6 80.2 %copy-start.28 = (f32[3072]{0:T(1024)S(1)}, f32[3072]{0:T(1024)}, u32[]{:S(2)}) copy-start(f32[3072]{0:T(1024)} %convert_element_type.131) | copy-start | bytes 36868
  123.4 201.7 %copy-start = (f32[1024,768]{1,0:T(8,128)}, f32[1024,768]{1,0:T(8,128)S(1)}, u32[]{:S(2)}) copy-start(f32[1024,768]{1,0:T(8,128)S(1)} %get-tuple-element.220) | copy-start | bytes 9437188
  123.4 201.7 %copy-start.11 = (f32[1024]{0:T(1024)}, f32[1024]{0:T(1024)S(1)}, u32[]{:S(2)}) copy-start(f32[1024]{0:T(1024)S(1)} %broadcast_multiply_fusion.1) | copy-start | bytes 12292
  123.9 201.2 %copy-start.13 = (f32[1024]{0:T(1024)}, f32[1024]{0:T(1024)S(1)}, u32[]{:S(2)}) copy-start(f32[1024]{0:T(1024)S(1)} %fusion.22) | copy-start | bytes 12292
  123.9 155.6 %copy-start.30 = (f32[768]{0:T(1024)S(1)}, f32[768]{0:T(1024)}, u32[]{:S(2)}) copy-start(f32[768]{0:T(1024)} %convert_element_type.133) | copy-start | bytes 9220
  279.6 9.5 %copy-start.2 = (bf16[2,512,768]{2,1,0:T(8,128)(2,1)S(1)}, bf16[2,512,768]{2,1,0:T(8,128)(2,1)}, u32[]{:S(2)}) copy-start(bf16[2,512,768]{2,1,0:T(8,128)(2,1)} %param.35) | copy-start | bytes 4718596
  279.6 9.5 %copy-start.21 = (f32[768]{0:T(1024)S(1)}, f32[768]{0:T(1024)}, u32[]{:S(2)}) copy-start(f32[768]{0:T(1024)} %convert_element_type.134) | copy-start | bytes 9220
  288.5 2.3 copy-start.24
  326.6 2.6 copy-start.34
  326.6 2.6 copy-start.22
  332.1 2.8 copy-start.10
  332.1 2.8 copy-start.18
  332.1 211.5 %reduce-scatter.13.cloned.1.call-start = ((), (), s32[]{:S(2)}) async-start(), calls=%async_computation.11 | async-start | bytes 7962624
  335.0 2.6 copy-start.6
  362.5 3.3 copy-start.7
  365.8 2.6 copy-start.6
  393.3 3.4 copy-start.7
  414.8 293.7 %reduce-scatter.9.cloned.1.call-start = ((), (), s32[]{:S(2)}) async-start(), calls=%async_computation.9 | async-start | bytes 10616832 | tf_op jit(solution)/shard_map/reduce_scatter | solution.py:170
  427.3 446.0 %reduce-scatter.11.cloned.1.call-start = ((), (), s32[]{:S(2)}) async-start(), calls=%async_computation.10 | async-start | bytes 10616832 | tf_op jit(solution)/shard_map/reduce_scatter | solution.py:171
  438.9 485.9 %all-reduce.4.cloned.1.call-start = ((), (), s32[]{:S(2)}) async-start(), calls=%async_computation.12 | async-start | bytes 3833856 | tf_op jit(solution)/shard_map/psum | solution.py:206
  444.2 431.3 %copy-start.5 = (f32[1024,768]{1,0:T(8,128)S(1)}, f32[1024,768]{1,0:T(8,128)}, u32[]{:S(2)}) copy-start(f32[1024,768]{1,0:T(8,128)} %copy-done.4) | copy-start | bytes 9437188
  444.2 431.3 %copy-start.23 = (f32[1024]{0:T(1024)S(1)}, f32[1024]{0:T(1024)}, u32[]{:S(2)}) copy-start(f32[1024]{0:T(1024)} %copy-done.22) | copy-start | bytes 12292
  (14 other events, 18.2 us)
Sparse Core Ops, SparseCore 0:
  10.2 67.3 all-gather.4
  79.7 39.8 all-gather.6
  121.8 78.0 all-gather.8
  201.9 77.6 all-gather.10
  332.2 67.9 reduce-scatter.6
  414.9 128.6 reduce-scatter.12
  547.2 161.2 reduce-scatter.8
  712.1 161.1 reduce-scatter.10
  877.1 47.7 all-reduce.3
where the time goes:
time: 944 us; the launch traced here: 940 us
  waiting for transfers between devices  603 us (64%)
  matrix products  173 us (18%)
  other arithmetic  55.7 us (6%)
  local copies, waits for them, and re-layouts  48.9 us (5%)
  blocking collectives  43.5 us (5%)
  between operations  14.5 us (2%)
    reduce_scatter x1, waiting for transfers between devices, body(): lax.psum_scatter(shrink_term, 'fsdp', scatter_dimension=0, tiled=True)  163 us
    reduce_scatter x1, waiting for transfers between devices, body(): lax.psum_scatter(expand_term, 'fsdp', scatter_dimension=0, tiled=True)  163 us
    all_gather x1, waiting for transfers between devices, body(): lax.all_gather(expand_weight, 'fsdp', axis=0, tiled=True)  75.9 us
    all_gather x1, waiting for transfers between devices, body(): lax.all_gather(joint_weight, 'fsdp', axis=0, tiled=True)  57.8 us
    unnamed x10, waiting for transfers between devices  56.7 us
    all_gather x1, waiting for transfers between devices, body(): lax.all_gather(shrink_weight, 'fsdp', axis=0, tiled=True)  43.8 us
    psum x1, blocking collectives, body(): lax.psum((vector_terms[0], vector_terms[1], vector_terms[2], vector_terms...  43.5 us
    psum x1, waiting for transfers between devices, body(): lax.psum(joint_part.astype(jnp.bfloat16), 'rep').astype(jnp.float32)  40.4 us
  transfers between devices with their start and end apart: 9, of which 8 were waited for; matrix products, arithmetic and copies ran while one was open for 22% of the time, Pallas kernels for 0%

commit v1 on v0

--- a/solution.py
+++ b/solution.py
@@ -203,7 +203,7 @@
         lax.psum_scatter(close_term, "fsdp", scatter_dimension=0, tiled=True),
     )
     joint_grad, close_grad, expand_grad, shrink_grad = (
-        lax.psum(joint_part.astype(jnp.bfloat16), "rep").astype(jnp.float32),
+        jnp.sum(lax.all_gather(joint_part.astype(jnp.bfloat16), "rep"), axis=0).astype(jnp.float32),
         lax.psum(close_part.astype(jnp.bfloat16), "rep").astype(jnp.float32),
         lax.psum(expand_part.astype(jnp.bfloat16), "rep").astype(jnp.float32),
         lax.psum(shrink_part.astype(jnp.bfloat16), "rep").astype(jnp.float32),

time: 944 us -> 1050 us (1.11)
  waiting for transfers between devices: 603 us -> 686 us
  matrix products: 173 us -> 192 us
    reduce_scatter x0 -> x1, waiting for transfers between devices: none -> 99.9 us  [body(): lax.psum_scatter(joint_term, 'fsdp', scatter_dimension=0, tiled=True)]
    unnamed x10, waiting for transfers between devices: 56.7 us -> 2.68 us
    reduce_scatter x1, waiting for transfers between devices: 0.01 us -> 25.2 us  [body(): lax.psum_scatter(close_term, 'fsdp', scatter_dimension=0, tiled=True)]
    all_gather x0 -> x1, waiting for transfers between devices: none -> 10.9 us  [body(): lax.all_gather(joint_part.astype(jnp.bfloat16), 'rep')]
  transfers between devices with their start and end apart: 9 -> 10, of which waited for: 8 -> 10; matrix products, arithmetic and copies ran while one was open for 22% -> 13% of each run, Pallas kernels for 0% -> 0%
where the time goes in v1:
time: 1050 us; the launch traced here: 1040 us
  waiting for transfers between devices  686 us (65%)
  matrix products  192 us (18%)
  other arithmetic  60 us (6%)
  local copies, waits for them, and re-layouts  47.9 us (5%)
  blocking collectives  41.3 us (4%)
  between operations  14.9 us (1%)
    reduce_scatter x1, waiting for transfers between devices, body(): lax.psum_scatter(expand_term, 'fsdp', scatter_dimension=0, tiled=True)  163 us
    reduce_scatter x1, waiting for transfers between devices, body(): lax.psum_scatter(shrink_term, 'fsdp', scatter_dimension=0, tiled=True)  163 us
    reduce_scatter x1, waiting for transfers between devices, body(): lax.psum_scatter(joint_term, 'fsdp', scatter_dimension=0, tiled=True)  99.9 us
    all_gather x1, waiting for transfers between devices, body(): lax.all_gather(expand_weight, 'fsdp', axis=0, tiled=True)  75.9 us
    all_gather x1, waiting for transfers between devices, body(): lax.all_gather(joint_weight, 'fsdp', axis=0, tiled=True)  57.8 us
    all_gather x1, waiting for transfers between devices, body(): lax.all_gather(shrink_weight, 'fsdp', axis=0, tiled=True)  43.7 us
    psum x1, blocking collectives, body(): lax.psum((vector_terms[0], vector_terms[1], vector_terms[2], vector_terms...  41.3 us
    psum x1, waiting for transfers between devices, body(): lax.psum(close_part.astype(jnp.bfloat16), 'rep').astype(jnp.float32)  40.4 us
  transfers between devices with their start and end apart: 10, of which 10 were waited for; matrix products, arithmetic and copies ran while one was open for 13% of the time, Pallas kernels for 0%

profile of v1, /device:TPU:0, one launch (start us, length us, event | category | flops | bytes accessed | tf_op | source)
XLA Modules:
  0.0 1043.6 jit_solution(5206604371495511188)
XLA Ops:
  19.7 57.8 %all-gather.7.cloned.1.call-done = bf16[768,2304]{1,0:T(8,128)(2,1)} async-done(((bf16[96,2304]{1,0:T(8,128)(2,1)}), bf16[768,2304]{1,0:T(8,128)(2,1)}) %all-gather.7.cloned.1.call-update) | async-done | bytes 3538960 | tf_op jit(solution)/shard_map/all_gather | solution.py:113
  77.5 8.5 add_convert_fusion.1
  86.1 6.9 copy.64
  93.0 23.5 %while.22 = (s32[]{:T(128)}, bf16[2,512,768]{2,1,0:T(8,128)(2,1)}, f32[2,12,512,1]{2,1,3,0:T(8,128)S(1)}, bf16[2,512,2304]{1,2,0:T(8,128)(2,1)}, s32[2,512]{1,0:T(2,128)S(1)}, /*index=5*/s32[]{:T(128)}) while((s32[]{:T(128)}, bf16[2,512,768]{2,1,0:T(8,128)(2,1)}, f32[2,12,512,1]{2,1,3,0:T(8,128)S(1)}, bf16[2,512,2304]{1,2,0:T(8,128)(2,1)}, ...), condition=%wide.region_3.4_spmd, body=%wide.region_0.3_spmd.sunk | while | flops 843311104 | bytes 54753872 | solution.py:121
  99.9 3.6 fusion.98
  119.6 3.8 fusion.33
  124.0 75.9 %all-gather.11.cloned.1.call-done = bf16[768,3072]{1,0:T(8,128)(2,1)} async-done(((bf16[96,3072]{1,0:T(8,128)(2,1)}), bf16[768,3072]{1,0:T(8,128)(2,1)}) %all-gather.11.cloned.1.call-update) | async-done | bytes 4718608 | tf_op jit(solution)/shard_map/all_gather | solution.py:126
  199.8 36.1 %multiply_convert_fusion.1 = (bf16[1024,3072]{1,0:T(8,128)(2,1)}, f32[1024,3072]{1,0:T(8,128)}, f32[1024,3072]{1,0:T(8,128)}) fusion(f32[3072]{0:T(1024)S(1)} %copy-done.28, bf16[768,3072]{1,0:T(8,128)(2,1)} %all-gather.11.cloned.1.call-done, f32[1024,768]{1,0:T(8,128)S(1)} %get-tuple-element.185, f32[768]{0:T(1024)S(1)} %copy-done.19, ...), kind=kOutput, calls=%fused_computation.34 | convolution fusion | flops 5043388416 | bytes 39348224 | tf_op jit(solution)/shard_map/dot_general | solution.py:137
  235.9 43.7 %all-gather.13.cloned.1.call-done = bf16[3072,768]{1,0:T(8,128)(2,1)} async-done(((bf16[384,768]{1,0:T(8,128)(2,1)}), bf16[3072,768]{1,0:T(8,128)(2,1)}) %all-gather.13.cloned.1.call-update) | async-done | bytes 4718608 | tf_op jit(solution)/shard_map/all_gather | solution.py:127
  279.6 8.9 fusion.34
  295.5 19.1 %convert_reduce_fusion = (f32[3072]{0:T(1024)}, bf16[1024,3072]{1,0:T(8,128)(2,1)}) fusion(f32[1024,3072]{1,0:T(8,128)} %get-tuple-element.172, bf16[1024,768]{1,0:T(8,128)(2,1)} %get-tuple-element.164, bf16[3072,768]{1,0:T(8,128)(2,1)} %all-gather.13.cloned.1.call-done, f32[1024,3072]{1,0:T(8,128)} %get-tuple-element.186, f32[3072]{0:T(1024)S(1)} %copy-done.28), kind=kOutput, calls=%fused_computation.32 | convolution fusion | flops 4885312512 | bytes 37773312 | tf_op jit(solution)/shard_map/td,fd->tf/dot_general | solution.py:161
  314.7 10.1 multiply_reduce_fusion.1
  331.1 86.2 %while.23 = (s32[]{:T(128)}, bf16[2,512,2304]{2,1,0:T(8,128)(2,1)}, bf16[2,512,2304]{1,2,0:T(8,128)(2,1)}, s32[2,512]{1,0:T(2,128)S(1)}, f32[2,12,512,1]{2,1,3,0...) while((s32[]{:T(128)}, bf16[2,512,2304]{2,1,0:T(8,128)(2,1)}, bf16[2,512,2304]{1,2,0:T(8,128)(2,1)}, ...), condition=%wide.region_14.15_spmd, body=%wide.region_12.14_spmd.sunk | while | flops 2069358592 | bytes 174242512 | solution.py:185
  333.3 6.4 fusion.110
  342.3 11.0 %multiply_reduce_fusion.6 = (f32[12,512]{1,0:T(8,128)S(1)}, f32[12,512,512]{1,2,0:T(8,128)}) fusion(f32[12,512,512]{1,2,0:T(8,128)} %fusion.110, f32[12,512]{1,0:T(8,128)S(1)} %dynamic-slice_bitcast_fusion.8, pred[512,512]{0,1:T(8,128)(4,1)S(1)} %broadcast_compare_fusion.5, bf16[512,12,64]{0,2,1:T(8,128)(2,1)S(1)} %bitcast.163, ...), kind=kOutput, calls=%fused_computation.14.clone.1 | convolution fusion | flops 418375680 | bytes 27049984 | tf_op jit(solution)/shard_map/while/body/eval_jaxpr/qhd,khd->hqk/dot_general | solution.py:62
  354.9 7.0 multiply_convert_fusion.3
  376.2 6.4 fusion.110
  385.2 11.0 %multiply_reduce_fusion.6 = (f32[12,512]{1,0:T(8,128)S(1)}, f32[12,512,512]{1,2,0:T(8,128)}) fusion(f32[12,512,512]{1,2,0:T(8,128)} %fusion.110, f32[12,512]{1,0:T(8,128)S(1)} %dynamic-slice_bitcast_fusion.8, pred[512,512]{0,1:T(8,128)(4,1)S(1)} %broadcast_compare_fusion.5, bf16[512,12,64]{0,2,1:T(8,128)(2,1)S(1)} %bitcast.163, ...), kind=kOutput, calls=%fused_computation.14.clone.1 | convolution fusion | flops 418375680 | bytes 27049984 | tf_op jit(solution)/shard_map/while/body/eval_jaxpr/qhd,khd->hqk/dot_general | solution.py:62
  397.8 7.0 multiply_convert_fusion.3
  417.2 9.7 convolution_bitcast_fusion
  426.9 8.0 copy.76
  435.1 4.9 fusion.36
  440.1 10.9 %fusion.24 = f32[768,3072]{1,0:T(8,128)} fusion(bf16[1024,3072]{1,0:T(8,128)(2,1)} %get-tuple-element.191, f32[1024,768]{1,0:T(8,128)S(1)} %copy-done.1, f32[768]{0:T(1024)S(1)} %copy-done.20, f32[768]{0:T(1024)S(1)} %copy-done.16, f32[1024]{0:T(1024)S(1)} %copy-done.14, f32[1024]{0:T(1024)S(1)} %copy-done.12), kind=kOutput, calls=%fused_computation.89 | convolution fusion | flops 4835770368 | bytes 18888704 | tf_op jit(solution)/shard_map/td,tf->df/dot_general | solution.py:163
  452.4 10.2 fusion.37
  462.7 99.9 %reduce-scatter.13.cloned.1.call-done = f32[96,2304]{1,0:T(8,128)} async-done(((f32[768,2304]{1,0:T(8,128)}), f32[96,2304]{1,0:T(8,128)}) %reduce-scatter.13.cloned.1.call-update) | async-done | bytes 884752 | tf_op jit(solution)/shard_map/reduce_scatter | solution.py:202
  569.0 41.3 %all-reduce = (f32[768]{0:T(1024)}, f32[768]{0:T(1024)}, f32[768]{0:T(1024)}, f32[768]{0:T(1024)}, f32[768]{0:T(1024)}, /*index=5*/f32[3072]{0:T(1024)}, f32[768]{0:T(1024)}, f32[768]{0:T(1024)}, f32[768]{0:T(1024)}) all-reduce(f32[768]{0:T(1024)S(1)} %get-tuple-element.123, ...), channel_id=1, replica_groups=mesh['fsdp'=8,'rep'=4] {'fsdp','rep'}, use_global_device_ids=true, to_apply=%region_18.19 | all-reduce | flops 9216 | bytes 73728 | tf_op jit(solution)/shard_map/psum | solution.py:233
  610.3 25.2 %reduce-scatter.7.cloned.1.call-done = f32[96,768]{1,0:T(8,128)} async-done(((f32[768,768]{1,0:T(8,128)}), f32[96,768]{1,0:T(8,128)}) %reduce-scatter.7.cloned.1.call-update) | async-done | bytes 294928 | tf_op jit(solution)/shard_map/reduce_scatter | solution.py:203
  637.2 163.3 %reduce-scatter.9.cloned.1.call-done = f32[96,3072]{1,0:T(8,128)} async-done(((f32[768,3072]{1,0:T(8,128)}), f32[96,3072]{1,0:T(8,128)}) %reduce-scatter.9.cloned.1.call-update) | async-done | bytes 1179664 | tf_op jit(solution)/shard_map/reduce_scatter | solution.py:170
  802.7 162.7 %reduce-scatter.11.cloned.1.call-done = f32[384,768]{1,0:T(8,128)} async-done(((f32[3072,768]{1,0:T(8,128)}), f32[384,768]{1,0:T(8,128)}) %reduce-scatter.11.cloned.1.call-update) | async-done | bytes 1179664 | tf_op jit(solution)/shard_map/reduce_scatter | solution.py:171
  967.5 9.0 add_add_fusion.4
  976.5 10.9 %all-gather.15.cloned.1.call-done = bf16[384,2304]{1,0:T(8,128)(2,1)} async-done(((bf16[96,2304]{1,0:T(8,128)(2,1)}), bf16[384,2304]{1,0:T(8,128)(2,1)}) %all-gather.15.cloned.1.call-update) | async-done | bytes 1769488 | tf_op jit(solution)/shard_map/all_gather | solution.py:206
  990.1 40.4 %all-reduce.4.cloned.1.call-done = (bf16[96,768]{1,0:T(8,128)(2,1)}, bf16[96,3072]{1,0:T(8,128)(2,1)}, bf16[384,768]{1,0:T(8,128)(2,1)}) async-done(((bf16[96,768]{1,0:T(8,128)(2,1)}, bf16[96,3072]{1,0:T(8,128)(2,1)}, bf16[384,768]{1,0:T(8,128)(2,1)}), (bf16[96,768]{1,0:T(8,128)(2,1)}, bf16[96,3072]{1,0:T(8,128)(2,1)}, bf16[384,768]{1,0:T(8,128)(2,1)})) %all-reduce.4.cloned.1.call-update) | async-done | bytes 1327120 | tf_op jit(solution)/shard_map/psum | solution.py:207
  (192 shorter events, 108.6 us)
Async XLA Ops:
  7.2 70.3 %all-gather.7.cloned.1.call-start = ((), (), s32[]{:S(2)}) async-start(), calls=%async_computation.4 | async-start | bytes 3981312 | tf_op jit(solution)/shard_map/all_gather | solution.py:113
  7.9 111.7 %all-gather.9.cloned.1.call-start = ((), (), s32[]{:S(2)}) async-start(), calls=%async_computation.5 | async-start | bytes 1327104 | tf_op jit(solution)/shard_map/all_gather | solution.py:114
  8.7 191.2 %all-gather.11.cloned.1.call-start = ((), (), s32[]{:S(2)}) async-start(), calls=%async_computation.6 | async-start | bytes 5308416 | tf_op jit(solution)/shard_map/all_gather | solution.py:126
  9.4 270.2 %all-gather.13.cloned.1.call-start = ((), (), s32[]{:S(2)}) async-start(), calls=%async_computation.7 | async-start | bytes 5308416 | tf_op jit(solution)/shard_map/all_gather | solution.py:127
  10.0 552.6 %reduce-scatter.13.cloned.1.call-start = ((), (), s32[]{:S(2)}) async-start(), calls=%async_computation.12 | async-start | bytes 7962624 | tf_op jit(solution)/shard_map/reduce_scatter | solution.py:202
  86.1 6.9 copy-start.17
  93.0 26.6 %copy-start.31 = (f32[768]{0:T(1024)S(1)}, f32[768]{0:T(1024)}, u32[]{:S(2)}) copy-start(f32[768]{0:T(1024)} %convert_element_type.129) | copy-start | bytes 9220
  119.6 80.2 %copy-start.15 = (f32[768]{0:T(1024)S(1)}, f32[768]{0:T(1024)}, u32[]{:S(2)}) copy-start(f32[768]{0:T(1024)} %convert_element_type.130) | copy-start | bytes 9220
  119.6 80.2 %copy-start.19 = (f32[768]{0:T(1024)S(1)}, f32[768]{0:T(1024)}, u32[]{:S(2)}) copy-start(f32[768]{0:T(1024)} %convert_element_type.131) | copy-start | bytes 9220
  119.6 80.2 %copy-start.28 = (f32[3072]{0:T(1024)S(1)}, f32[3072]{0:T(1024)}, u32[]{:S(2)}) copy-start(f32[3072]{0:T(1024)} %convert_element_type.133) | copy-start | bytes 36868
  123.4 201.4 %copy-start = (f32[1024,768]{1,0:T(8,128)}, f32[1024,768]{1,0:T(8,128)S(1)}, u32[]{:S(2)}) copy-start(f32[1024,768]{1,0:T(8,128)S(1)} %get-tuple-element.185) | copy-start | bytes 9437188
  123.4 201.4 %copy-start.11 = (f32[1024]{0:T(1024)}, f32[1024]{0:T(1024)S(1)}, u32[]{:S(2)}) copy-start(f32[1024]{0:T(1024)S(1)} %broadcast_multiply_fusion.1) | copy-start | bytes 12292
  123.9 200.9 %copy-start.13 = (f32[1024]{0:T(1024)}, f32[1024]{0:T(1024)S(1)}, u32[]{:S(2)}) copy-start(f32[1024]{0:T(1024)S(1)} %fusion.22) | copy-start | bytes 12292
  123.9 155.6 %copy-start.30 = (f32[768]{0:T(1024)S(1)}, f32[768]{0:T(1024)}, u32[]{:S(2)}) copy-start(f32[768]{0:T(1024)} %convert_element_type.135) | copy-start | bytes 9220
  279.6 9.5 copy-start.2
  279.6 9.5 copy-start.21
  333.3 6.7 copy-start.6
  342.3 11.0 %slice-start = ((s8[12582912]{0:T(1024)(128)(4,1)}), s8[4194304]{0:T(1024)(128)(4,1)S(1)}, s32[]{:S(2)}) async-start(s8[12582912]{0:T(1024)(128)(4,1)} %bitcast.153), calls=%async_computation.14 | async-start | bytes 8388608 | tf_op jit(solution)/shard_map/while
  342.3 11.0 %slice-start.1 = ((s8[12582912]{0:T(1024)(128)(4,1)}), s8[4194304]{0:T(1024)(128)(4,1)S(1)}, s32[]{:S(2)}) async-start(s8[12582912]{0:T(1024)(128)(4,1)} %bitcast.153), calls=%async_computation.15 | async-start | bytes 8388608 | tf_op jit(solution)/shard_map/while
  342.3 12.6 %slice-start.2 = ((s8[12582912]{0:T(1024)(128)(4,1)}), s8[4194304]{0:T(1024)(128)(4,1)S(1)}, s32[]{:S(2)}) async-start(s8[12582912]{0:T(1024)(128)(4,1)} %bitcast.153), calls=%async_computation.16 | async-start | bytes 8388608 | tf_op jit(solution)/shard_map/while
  376.1 6.7 copy-start.6
  385.2 11.0 %slice-start = ((s8[12582912]{0:T(1024)(128)(4,1)}), s8[4194304]{0:T(1024)(128)(4,1)S(1)}, s32[]{:S(2)}) async-start(s8[12582912]{0:T(1024)(128)(4,1)} %bitcast.153), calls=%async_computation.14 | async-start | bytes 8388608 | tf_op jit(solution)/shard_map/while
  385.2 11.0 %slice-start.1 = ((s8[12582912]{0:T(1024)(128)(4,1)}), s8[4194304]{0:T(1024)(128)(4,1)S(1)}, s32[]{:S(2)}) async-start(s8[12582912]{0:T(1024)(128)(4,1)} %bitcast.153), calls=%async_computation.15 | async-start | bytes 8388608 | tf_op jit(solution)/shard_map/while
  385.2 12.6 %slice-start.2 = ((s8[12582912]{0:T(1024)(128)(4,1)}), s8[4194304]{0:T(1024)(128)(4,1)S(1)}, s32[]{:S(2)}) async-start(s8[12582912]{0:T(1024)(128)(4,1)} %bitcast.153), calls=%async_computation.16 | async-start | bytes 8388608 | tf_op jit(solution)/shard_map/while
  435.0 200.6 %reduce-scatter.7.cloned.1.call-start = ((), (), s32[]{:S(2)}) async-start(), calls=%async_computation.8 | async-start | bytes 2654208 | tf_op jit(solution)/shard_map/reduce_scatter | solution.py:203
  440.0 360.5 %reduce-scatter.9.cloned.1.call-start = ((), (), s32[]{:S(2)}) async-start(), calls=%async_computation.9 | async-start | bytes 10616832 | tf_op jit(solution)/shard_map/reduce_scatter | solution.py:170
  451.1 514.3 %reduce-scatter.11.cloned.1.call-start = ((), (), s32[]{:S(2)}) async-start(), calls=%async_computation.10 | async-start | bytes 10616832 | tf_op jit(solution)/shard_map/reduce_scatter | solution.py:171
  462.6 102.3 %copy-start.3 = (bf16[2,512,768]{2,1,0:T(8,128)(2,1)S(1)}, bf16[2,512,768]{2,1,0:T(8,128)(2,1)}, u32[]{:S(2)}) copy-start(bf16[2,512,768]{2,1,0:T(8,128)(2,1)} %param.35) | copy-start | bytes 4718596
  462.7 524.7 %all-gather.15.cloned.1.call-start = ((), (), s32[]{:S(2)}) async-start(), calls=%async_computation.11 | async-start | bytes 2211840 | tf_op jit(solution)/shard_map/all_gather | solution.py:206
  564.6 465.9 %all-reduce.4.cloned.1.call-start = ((), (), s32[]{:S(2)}) async-start(), calls=%async_computation.13 | async-start | bytes 2654208 | tf_op jit(solution)/shard_map/psum | solution.py:207
  568.3 399.2 %copy-start.5 = (f32[1024,768]{1,0:T(8,128)S(1)}, f32[1024,768]{1,0:T(8,128)}, u32[]{:S(2)}) copy-start(f32[1024,768]{1,0:T(8,128)} %copy-done.4) | copy-start | bytes 9437188
  568.3 399.2 %copy-start.23 = (f32[1024]{0:T(1024)S(1)}, f32[1024]{0:T(1024)}, u32[]{:S(2)}) copy-start(f32[1024]{0:T(1024)} %copy-done.22) | copy-start | bytes 12292
  (20 other events, 57.4 us)
Sparse Core Ops, SparseCore 0:
  10.2 67.3 all-gather.6
  79.7 39.8 all-gather.8
  121.8 78.0 all-gather.10
  201.9 77.6 all-gather.12
  435.1 127.4 reduce-scatter.12
  566.0 69.5 reduce-scatter.6
  639.2 161.3 reduce-scatter.8
  804.1 161.1 reduce-scatter.10
  967.5 19.8 all-gather.14
  990.9 39.5 all-reduce.3
